TPU v7x, 32 devices: a whole 2x2x4 slice. The times are simulated.
32 devices in a mesh: grp: 2 (over y), cls: 8 (over z, x), img: 2 (over core).
Axes of the slice: x: 2, y: 2, z: 4, core: 2. Of those that a mesh axis runs over, the one named last changes fastest.
Arguments:
- embeddings: bfloat16 [4096, 1536], P(('grp', 'img'), 'cls'), parts along dimension 0, may hold values from -6 to 6, as said below
- labels: int32 [4096], P(('grp', 'img')), parts along dimension 0, may hold values from 0 to 1023
- weights: float32 [3072, 1024], P(('grp', 'img'), 'cls'), parts along dimension 0, may hold values from -12 to 12, as said below
- strength: int32 [2], P('grp'), parts along dimension 0, may hold values from 0 to 3
Outputs:
- new_weights: float32 [3072, 1024], P(('grp', 'img'), 'cls'), parts along dimension 0
- losses: float32 [4096], P(('grp', 'img')), parts along dimension 0
There are 2 independent parts, one for each index of `grp`. A program takes and returns all parts, laid end to end along the dimension named above; each array names one. Nothing has to cross between parts.
Inputs may be any that keep to these rules, and one draw needn't show every extreme that they name: embeddings of order one. Initial probe weights of order a few.
All inputs are finite; a program needn't handle non-finite values.
Results may differ from a plain program's by a relative error of at most 0.0032.
Values may be sent and summed in bfloat16 or wider, within the bound.
A program may use at most 64 MiB of HBM per device.

v0:
```python
import math

import jax
import jax.numpy as jnp
from jax import lax
from jax.sharding import PartitionSpec as P

D = 1536
ITERS = 2


def shrink(master, grad, lam):
    moved = master - 16.0 * grad
    return jnp.sign(moved) * jnp.maximum(jnp.abs(moved) - lam, 0.0)


def shards(embeddings, labels, weights, strength):
    scale = 1.0 / math.sqrt(D)
    lam = 16.0 * 0.01 * jnp.exp2(strength[0].astype(jnp.float32))
    full_x = lax.all_gather(embeddings, "cls", axis=1, tiled=True)
    cls_width = weights.shape[1]
    first_class = lax.axis_index("cls") * cls_width
    classes = first_class + lax.iota(jnp.int32, cls_width)
    onehot = (labels[:, None] == classes[None, :]).astype(jnp.float32)
    master = lax.all_gather(weights, "img", axis=0, tiled=True)
    operand = master.astype(jnp.bfloat16)
    losses = jnp.zeros((labels.shape[0],), jnp.float32)
    for step in range(ITERS):
        logits = jnp.dot(full_x, operand, preferred_element_type=jnp.float32) * scale
        local_top = jnp.max(logits, axis=1)
        label_term = jnp.sum(logits * onehot, axis=1)
        top = lax.pmax(local_top, "cls")
        total, picked = lax.psum(
            (jnp.sum(jnp.exp(logits - top[:, None]), axis=1), label_term), "cls"
        )
        lse = top + jnp.log(total)
        losses = lse - picked
        resid = (jnp.exp(logits - lse[:, None]) - onehot).astype(jnp.bfloat16)
        grad_local = (
            lax.dot_general(
                full_x, resid, (((0,), (0,)), ((), ())), preferred_element_type=jnp.float32
            )
            * scale
        )
        grad = lax.psum(grad_local, "img")
        master = shrink(master, grad, lam)
        operand = master.astype(jnp.bfloat16)
    rows = weights.shape[0]
    new_weights = lax.dynamic_slice_in_dim(master, lax.axis_index("img") * rows, rows, 0)
    return (new_weights, losses)


def solution(mesh):
    placed = (P(("grp", "img"), "cls"), P(("grp", "img")), P(("grp", "img"), "cls"), P("grp"))
    return jax.shard_map(
        shards,
        mesh=mesh,
        in_specs=placed,
        out_specs=(P(("grp", "img"), "cls"), P(("grp", "img"))),
        check_vma=False,
    )
```

profile of v0, /device:TPU:1, one launch (start us, length us, event | category | flops | bytes accessed | tf_op | source)
XLA Modules:
  0.0 210.0 jit_solution(16586278713644996422)
XLA Ops:
  7.2 0.0 all-gather.2.cloned.1.call-start
  7.2 0.7 all-gather.2.cloned.1.call-update
  7.9 0.0 all-reduce.4.cloned.1.call-start
  7.9 1.2 copy.6
  9.1 2.5 %all_gather.6 = f32[1536,128]{0,1:T(8,128)} all-gather(f32[768,128]{0,1:T(8,128)S(1)} %copy.6), channel_id=1, replica_groups=mesh['grp'=2,'cls'=8,'img'=2] {'img'}, dimensions={0}, use_global_device_ids=true | all-gather | bytes 1179648 | tf_op jit(solution)/shard_map/all_gather | solution.py:25
  11.6 60.3 %all-gather.2.cloned.1.call-done = bf16[1024,1536]{0,1:T(8,128)(2,1)} async-done(((bf16[1024,192]{0,1:T(8,128)(2,1)}), bf16[1024,1536]{0,1:T(8,128)(2,1)}) %all-gather.2.cloned.1.call-update) | async-done | bytes 3145744 | tf_op jit(solution)/shard_map/all_gather | solution.py:20
  71.9 3.7 %fusion.19 = (f32[1024]{0:T(1024)S(1)}, f32[1024,128]{0,1:T(8,128)}) fusion(bf16[1024,1536]{0,1:T(8,128)(2,1)} %all-gather.2.cloned.1.call-done, f32[1536,128]{0,1:T(8,128)} %all_gather.6), kind=kOutput, calls=%fused_computation.34 | convolution fusion | flops 403110912 | bytes 4460544 | tf_op jit(solution)/shard_map/dot_general | solution.py:29
  75.6 16.2 %pmax.14 = f32[1024]{0:T(1024)S(1)} all-reduce(f32[1024]{0:T(1024)S(1)} %get-tuple-element.10), channel_id=1, replica_groups=mesh['grp'=2,'cls'=8,'img'=2] {'cls'}, use_global_device_ids=true, to_apply=%region_1.0 | all-reduce | flops 1024 | bytes 8192 | tf_op jit(solution)/shard_map/pmax | solution.py:32
  91.8 1.1 exponential_reduce_fusion
  92.9 13.7 %psum.35 = f32[1024]{0:T(1024)S(1)} all-reduce(f32[1024]{0:T(1024)S(1)} %exponential_reduce_fusion), channel_id=1, replica_groups=mesh['grp'=2,'cls'=8,'img'=2] {'cls'}, use_global_device_ids=true, to_apply=%region_3.0 | all-reduce | flops 1024 | bytes 8192 | tf_op jit(solution)/shard_map/psum | solution.py:33
  106.6 3.1 %fusion = f32[1536,128]{0,1:T(8,128)} fusion(bf16[1024,1536]{0,1:T(8,128)(2,1)S(1)} %copy-done, f32[1024,128]{0,1:T(8,128)} %get-tuple-element.11, s32[1024]{0:T(1024)S(1)} %copy-done.2, f32[1024]{0:T(1024)S(1)} %log_add_fusion.1, s32[128]{0:T(128)S(1)} %iota_add_fusion), kind=kOutput, calls=%fused_computation.2 | convolution fusion | flops 403505152 | bytes 4465152 | tf_op jit(solution)/shard_map/dot_general | solution.py:40
  109.7 0.0 all-reduce.6.cloned.1.call-start
  110.5 24.9 %all-reduce.4.cloned.1.call-done = f32[1536,128]{0,1:T(8,128)} async-done(((f32[1536,128]{0,1:T(8,128)}), f32[1536,128]{0,1:T(8,128)}) %all-reduce.4.cloned.1.call-update) | async-done | bytes 786448 | tf_op jit(solution)/shard_map/psum | solution.py:45
  135.3 1.7 maximum_multiply_fusion
  137.1 0.9 copy-done.1
  137.9 1.4 fusion.20
  139.3 17.9 %pmax.15 = f32[1024]{0:T(1024)S(1)} all-reduce(f32[1024]{0:T(1024)S(1)} %get-tuple-element.12), channel_id=1, replica_groups=mesh['grp'=2,'cls'=8,'img'=2] {'cls'}, use_global_device_ids=true, to_apply=%region_6.0 | all-reduce | flops 1024 | bytes 8192 | tf_op jit(solution)/shard_map/pmax | solution.py:32
  157.2 1.2 fusion.2
  158.4 13.9 %all-reduce = (f32[1024]{0:T(1024)S(1)}, f32[1024]{0:T(1024)S(1)}) all-reduce(f32[1024]{0:T(1024)S(1)} %get-tuple-element.5, f32[1024]{0:T(1024)S(1)} %get-tuple-element.4), channel_id=1, replica_groups=mesh['grp'=2,'cls'=8,'img'=2] {'cls'}, use_global_device_ids=true, to_apply=%region_8.0 | all-reduce | flops 2048 | bytes 16384 | tf_op jit(solution)/shard_map/psum | solution.py:33
  172.3 0.6 fusion.18
  172.9 3.1 %fusion.1 = f32[1536,128]{0,1:T(8,128)} fusion(bf16[1024,1536]{0,1:T(8,128)(2,1)S(1)} %copy-done, f32[128,1024]{1,0:T(8,128)} %get-tuple-element.13, f32[1024]{0:T(1024)S(1)} %get-tuple-element.9, s32[1024]{0:T(1024)S(1)} %copy-done.2, s32[128]{0:T(128)S(1)} %iota_add_fusion), kind=kOutput, calls=%fused_computation.3 | convolution fusion | flops 403505152 | bytes 4465152 | tf_op jit(solution)/shard_map/dot_general | solution.py:40
  176.1 25.2 %all-reduce.6.cloned.1.call-done = f32[1536,128]{0,1:T(8,128)} async-done(((f32[1536,128]{0,1:T(8,128)}), f32[1536,128]{0,1:T(8,128)}) %all-reduce.6.cloned.1.call-update) | async-done | bytes 786448 | tf_op jit(solution)/shard_map/psum | solution.py:45
  201.3 1.3 maximum_multiply_fusion.1
  202.6 0.9 copy.7
  (9 shorter events, 0.1 us)
Async XLA Ops:
  7.2 64.7 %all-gather.2.cloned.1.call-start = ((), (), s32[]{:S(2)}) async-start(), calls=%async_computation | async-start | bytes 3538944 | tf_op jit(solution)/shard_map/all_gather | solution.py:20
  7.9 127.4 %all-reduce.4.cloned.1.call-start = ((), (), s32[]{:S(2)}) async-start(), calls=%async_computation.1 | async-start | bytes 1572864 | tf_op jit(solution)/shard_map/psum | solution.py:45
  9.1 97.5 %copy-start.2 = (s32[1024]{0:T(1024)S(1)}, s32[1024]{0:T(1024)}, u32[]{:S(2)}) copy-start(s32[1024]{0:T(1024)} %param.5) | copy-start | bytes 12292
  71.9 34.7 %copy-start = (bf16[1024,1536]{0,1:T(8,128)(2,1)S(1)}, bf16[1024,1536]{0,1:T(8,128)(2,1)}, u32[]{:S(2)}) copy-start(bf16[1024,1536]{0,1:T(8,128)(2,1)} %all-gather.2.cloned.1.call-done) | copy-start | bytes 9437188
  109.7 91.6 %all-reduce.6.cloned.1.call-start = ((), (), s32[]{:S(2)}) async-start(), calls=%async_computation.2 | async-start | bytes 1572864 | tf_op jit(solution)/shard_map/psum | solution.py:45
  137.1 0.9 copy-start.1
Sparse Core Ops, SparseCore 0:
  10.2 61.6 all-gather.1
  109.9 25.4 all-reduce.3
  176.2 25.0 all-reduce.5
where the time goes:
time: 211 us; the launch traced here: 210 us
  waiting for transfers between devices  111 us (53%)
  blocking collectives  64.2 us (30%)
  between operations  14.5 us (7%)
  matrix products  11.3 us (5%)
  other arithmetic  5.92 us (3%)
  local copies, waits for them, and re-layouts  2.95 us (1%)
    all_gather x1, waiting for transfers between devices, shards(): full_x = lax.all_gather(embeddings, 'cls', axis=1, tiled=True)  60.3 us
    psum x2, waiting for transfers between devices, shards(): grad = lax.psum(grad_local, 'img')  50.1 us
    pmax x2, blocking collectives, shards(): top = lax.pmax(local_top, 'cls')  34.1 us
    psum x2, blocking collectives, shards(): lax.psum((jnp.sum(jnp.exp(logits - top[:, None]), axis=1), label_term), '...  27.6 us
    dot_general x2, matrix products, shards(): lax.dot_general(full_x, resid, (((0,), (0,)), ((), ())), preferred_elemen...  6.26 us
    dot_general x2, matrix products, shards(): jnp.dot(full_x, operand, preferred_element_type=jnp.float32) * scale  5.05 us
  transfers between devices with their start and end apart: 3, of which 3 were waited for; matrix products, arithmetic and copies ran while one was open for 1% of the time, Pallas kernels for 0%

commit v1 on v0

--- a/solution.py
+++ b/solution.py
@@ -1,12 +1,24 @@
+import functools
 import math
 
 import jax
 import jax.numpy as jnp
 from jax import lax
+from jax.experimental import pallas as pl
+from jax.experimental.pallas import tpu as pltpu
 from jax.sharding import PartitionSpec as P
 
 D = 1536
 ITERS = 2
+MESH = pl.DeviceIdType.MESH
+SCALE = 1.0 / math.sqrt(D)
+
+NX, NZ = 2, 4
+N = NX * NZ
+IMGS, WIDTH, CLS = 1024, 192, 128
+UP, DOWN, ACROSS = 0, 1, 2
+MAIN, TAIL_A, TAIL_B = 0, 1, 2
+CHUNK = 256
 
 
 def shrink(master, grad, lam):
@@ -14,8 +26,301 @@
     return jnp.sign(moved) * jnp.maximum(jnp.abs(moved) - lam, 0.0)
 
 
-def shards(embeddings, labels, weights, strength):
-    scale = 1.0 / math.sqrt(D)
+def nt(a, b):
+    return lax.dot_general(a, b, (((1,), (1,)), ((), ())), preferred_element_type=jnp.float32)
+
+
+def kernel(x_ref, lab_ref, w_ref, s_ref, out_ref, loss_ref,
+           xd, tp, wb, wb2, master, acc, ex, resid, gsend, grecv, lses, picks,
+           send_sem, recv_sem, w_send, w_recv, g_send, g_recv, l_send, l_recv):
+    me = lax.axis_index("cls")
+    img = lax.axis_index("img")
+    grp = lax.axis_index("grp")
+    z, x = me // NX, me % NX
+    mate = (grp, me, 1 - img)
+
+    barrier = pltpu.get_barrier_semaphore()
+    for k in range(1, N):
+        pl.semaphore_signal(barrier, inc=1, device_id=(grp, (me + k) % N, img), device_id_type=MESH)
+    pl.semaphore_signal(barrier, inc=1, device_id=mate, device_id_type=MESH)
+    pl.semaphore_wait(barrier, N)
+
+    def main_tile(sz, sx):
+        return (sz // 2) * 6 + (sz % 2) * 2 + sx
+
+    def tail_tile(sz):
+        return (sz // 2) * 6 + 4 + sz % 2
+
+    def place(sz, sx, q):
+        if q == MAIN:
+            return xd.at[main_tile(sz, sx)]
+        if q == TAIL_A:
+            return tp.at[sz * NX + sx, pl.ds(0, 256)]
+        return tp.at[sz * NX + sx, pl.ds(256, 256)]
+
+    def copy(sz, sx, q, way, src=None):
+        to = {UP: me + NX, DOWN: me - NX, ACROSS: z * NX + 1 - x}[way]
+        ref = place(sz, sx, q)
+        return pltpu.make_async_remote_copy(
+            src_ref=ref if src is None else src,
+            dst_ref=ref,
+            send_sem=send_sem.at[way, sz * NX + sx, q],
+            recv_sem=recv_sem.at[sz * NX + sx, q],
+            device_id=(grp, to, img),
+            device_id_type=MESH,
+        )
+
+    started = []
+
+    def send(cond, *args, **kw):
+        @pl.when(cond)
+        def _():
+            copy(*args, **kw).start()
+        started.append((cond, args, kw))
+
+    def arrived(sz, sx, q):
+        copy(sz, sx, q, ACROSS).wait_recv()
+
+    yes = z >= 0
+    own = dict(src=x_ref.at[:, pl.ds(0, 128)])
+    send(yes, z, x, MAIN, ACROSS, **own)
+    send(z < NZ - 1, z, x, MAIN, UP, **own)
+    send(z > 0, z, x, MAIN, DOWN, **own)
+    tp[me] = jnp.concatenate([x_ref[0:512, 128:192], x_ref[512:1024, 128:192]], axis=1)
+    for q in (TAIL_B, TAIL_A):
+        send(yes, z, x, q, ACROSS)
+        send(z < NZ - 1, z, x, q, UP)
+        send(z > 0, z, x, q, DOWN)
+    xd[main_tile(z, x)] = x_ref[:, 0:128]
+
+    order = [(192 * k, 128) for k in range(4)] + [(192 * k + 128, 64) for k in range(4)]
+    rows = jnp.concatenate([w_ref[a:a + n] for a, n in order], axis=0)
+    for j in range(3):
+        part = rows[256 * j:256 * j + 256].T
+        master[j] = part
+        wb[img * 3 + j] = part.astype(jnp.bfloat16)
+
+    def weights_copy(buf, step):
+        half = buf.at[pl.ds(img * 3, 3)]
+        return pltpu.make_async_remote_copy(
+            src_ref=half, dst_ref=half, send_sem=w_send.at[step], recv_sem=w_recv.at[step],
+            device_id=mate, device_id_type=MESH)
+
+    def weights_arrived(buf, step):
+        half = buf.at[pl.ds((1 - img) * 3, 3)]
+        pltpu.make_async_remote_copy(
+            src_ref=half, dst_ref=half, send_sem=w_send.at[step], recv_sem=w_recv.at[step],
+            device_id=mate, device_id_type=MESH).wait_recv()
+
+    weights_copy(wb, 0).start()
+    acc[...] = jnp.zeros_like(acc)
+
+    def block(g, r=slice(None)):
+        return jnp.concatenate([xd[2 * g, r], xd[2 * g + 1, r]], axis=1)
+
+    def add_group(buf, g):
+        for n in range(0, IMGS, CHUNK):
+            r = slice(n, n + CHUNK)
+            acc[:, r] += nt(buf[g], block(g, r))
+
+    def finish(sz):
+        arrived(sz, 1 - x, MAIN)
+        add_group(wb, (sz // 2) * 3 + sz % 2)
+
+    def tails(sz):
+        lo, hi = tp[sz * NX], tp[sz * NX + 1]
+        t = tail_tile(sz)
+        xd[t, 0:512] = jnp.concatenate([lo[:, :64], hi[:, :64]], axis=1)
+        xd[t, 512:1024] = jnp.concatenate([lo[:, 64:], hi[:, 64:]], axis=1)
+
+    arrived(z, 1 - x, TAIL_B)
+    send(z < NZ - 1, z, 1 - x, TAIL_B, UP)
+    send(z > 0, z, 1 - x, TAIL_B, DOWN)
+
+    for d in range(NZ):
+        if d > 0:
+            for sz, here, way, onward in (
+                (z - d, z >= d, UP, z < NZ - 1),
+                (z + d, z + d < NZ, DOWN, z > 0),
+            ):
+                @pl.when(here)
+                def _(sz=sz):
+                    arrived(sz, x, MAIN)
+                both = jnp.logical_and(here, onward)
+                send(both, sz, x, MAIN, way)
+                send(here, sz, x, MAIN, ACROSS)
+            for sz, here, way, onward in (
+                (z - d, z >= d, UP, z < NZ - 1),
+                (z + d, z + d < NZ, DOWN, z > 0),
+            ):
+                both = jnp.logical_and(here, onward)
+                for sx, q in ((x, TAIL_B), (x, TAIL_A), (1 - x, TAIL_B)):
+                    @pl.when(here)
+                    def _(sz=sz, sx=sx, q=q):
+                        arrived(sz, sx, q)
+                    send(both, sz, sx, q, way)
+                send(here, sz, x, TAIL_A, ACROSS)
+        if d == 0:
+            pass
+        elif d == 1:
+            weights_arrived(wb, 0)
+            finish(z)
+        else:
+            for sz, here in ((z - d + 1, z >= d - 1), (z + d - 1, z + d - 1 < NZ)):
+                @pl.when(here)
+                def _(sz=sz):
+                    finish(sz)
+    for sz, here in ((z - NZ + 1, z >= NZ - 1), (z + NZ - 1, z == 0)):
+        @pl.when(here)
+        def _(sz=sz):
+            finish(sz)
+    for sz in range(NZ):
+        arrived(sz, 1 - x, TAIL_A)
+    for sz in range(NZ):
+        tails(sz)
+    for h in range(2):
+        add_group(wb, h * 3 + 2)
+
+    lam = 0.16 * jnp.exp2(s_ref[...].astype(jnp.float32))
+    first = me * CLS
+
+    def stat_copy(buf, sems, step, k):
+        return pltpu.make_async_remote_copy(
+            src_ref=buf.at[me], dst_ref=buf.at[me],
+            send_sem=l_send.at[sems, k], recv_sem=l_recv.at[sems, me],
+            device_id=(grp, (me + k) % N, img), device_id_type=MESH)
+
+    def stat_arrived(buf, sems, k):
+        frm = (me + k) % N
+        pltpu.make_async_remote_copy(
+            src_ref=buf.at[frm], dst_ref=buf.at[frm],
+            send_sem=l_send.at[sems, k], recv_sem=l_recv.at[sems, frm],
+            device_id=(grp, frm, img), device_id_type=MESH).wait_recv()
+
+    def grad_copy(step, j):
+        return pltpu.make_async_remote_copy(
+            src_ref=gsend.at[step, j], dst_ref=grecv.at[step, j],
+            send_sem=g_send.at[step, j], recv_sem=g_recv.at[step, j],
+            device_id=mate, device_id_type=MESH)
+
+    for step in range(ITERS):
+        last = step == ITERS - 1
+        tops = []
+        lse_buf = lses.at[step]
+        for n in range(0, IMGS, CHUNK):
+            r = slice(n, n + CHUNK)
+            logits = acc[:, r] * SCALE
+            top = jnp.max(logits, axis=0, keepdims=True)
+            e = jnp.exp(logits - top)
+            ex[:, r] = e
+            lse_buf[me, :, r] = top + jnp.log(jnp.sum(e, axis=0, keepdims=True))
+            tops.append(top)
+            if last:
+                hot = lab_ref[:, r] == first + lax.broadcasted_iota(jnp.int32, (CLS, CHUNK), 0)
+                picks[me, :, r] = jnp.sum(jnp.where(hot, logits, 0.0), axis=0, keepdims=True)
+        for k in range(1, N):
+            stat_copy(lse_buf, step, step, k).start()
+        if last:
+            for k in range(1, N):
+                stat_copy(picks, 2, step, k).start()
+        for k in range(1, N):
+            stat_arrived(lse_buf, step, k)
+        for n in range(0, IMGS, CHUNK):
+            r = slice(n, n + CHUNK)
+            parts = [lse_buf[k, :, r] for k in range(N)]
+            top = functools.reduce(jnp.maximum, parts)
+            lse = top + jnp.log(sum(jnp.exp(p - top) for p in parts))
+            if last:
+                loss_ref[:, r] = lse
+            hot = lab_ref[:, r] == first + lax.broadcasted_iota(jnp.int32, (CLS, CHUNK), 0)
+            prob = ex[:, r] * jnp.exp(tops[n // CHUNK] - lse)
+            resid[:, r] = (prob - jnp.where(hot, 1.0, 0.0)).astype(jnp.bfloat16)
+        for j in range(3):
+            gsend[step, j] = jnp.dot(
+                resid[...], block((1 - img) * 3 + j), preferred_element_type=jnp.float32)
+            grad_copy(step, j).start()
+        for j in range(3):
+            grad = jnp.dot(resid[...], block(img * 3 + j), preferred_element_type=jnp.float32)
+            grad_copy(step, j).wait_recv()
+            moved = master[j] - 16.0 * ((grad + grecv[step, j]) * SCALE)
+            new = moved - jnp.clip(moved, -lam, lam)
+            master[j] = new
+            if not last:
+                wb2[img * 3 + j] = new.astype(jnp.bfloat16)
+        if not last:
+            weights_copy(wb2, 1).start()
+            acc[...] = jnp.zeros_like(acc)
+            for j in range(3):
+                add_group(wb2, img * 3 + j)
+            weights_arrived(wb2, 1)
+            for j in range(3):
+                add_group(wb2, (1 - img) * 3 + j)
+
+    at = 0
+    new_rows = jnp.concatenate([master[j].T for j in range(3)], axis=0)
+    for a, n in order:
+        out_ref[a:a + n] = new_rows[at:at + n]
+        at += n
+    for k in range(1, N):
+        stat_arrived(picks, 2, k)
+    loss_ref[...] = loss_ref[...] - sum(picks[k] for k in range(N))
+
+    for cond, args, kw in started:
+        @pl.when(cond)
+        def _(args=args, kw=kw):
+            copy(*args, **kw).wait_send()
+    weights_copy(wb, 0).wait_send()
+    weights_copy(wb2, 1).wait_send()
+    for step in range(ITERS):
+        for j in range(3):
+            grad_copy(step, j).wait_send()
+        for k in range(1, N):
+            stat_copy(lses.at[step], step, step, k).wait_send()
+    for k in range(1, N):
+        stat_copy(picks, 2, 1, k).wait_send()
+
+
+def fused(embeddings, labels, weights, strength):
+    vmem = pl.BlockSpec(memory_space=pltpu.VMEM)
+    f32, bf16 = jnp.float32, jnp.bfloat16
+    new_weights, losses = pl.pallas_call(
+        kernel,
+        out_shape=(
+            jax.ShapeDtypeStruct((768, CLS), f32),
+            jax.ShapeDtypeStruct((1, IMGS), f32),
+        ),
+        in_specs=[vmem] * 4,
+        out_specs=(vmem, vmem),
+        scratch_shapes=[
+            pltpu.VMEM((12, IMGS, 128), bf16),
+            pltpu.VMEM((N, 512, 128), bf16),
+            pltpu.VMEM((6, CLS, 256), bf16),
+            pltpu.VMEM((6, CLS, 256), bf16),
+            pltpu.VMEM((3, CLS, 256), f32),
+            pltpu.VMEM((CLS, IMGS), f32),
+            pltpu.VMEM((CLS, IMGS), f32),
+            pltpu.VMEM((CLS, IMGS), bf16),
+            pltpu.VMEM((ITERS, 3, CLS, 256), f32),
+            pltpu.VMEM((ITERS, 3, CLS, 256), f32),
+            pltpu.VMEM((ITERS, N, 1, IMGS), f32),
+            pltpu.VMEM((N, 1, IMGS), f32),
+            pltpu.SemaphoreType.DMA((3, N, 3)),
+            pltpu.SemaphoreType.DMA((N, 3)),
+            pltpu.SemaphoreType.DMA((2,)),
+            pltpu.SemaphoreType.DMA((2,)),
+            pltpu.SemaphoreType.DMA((2, 3)),
+            pltpu.SemaphoreType.DMA((2, 3)),
+            pltpu.SemaphoreType.DMA((3, N)),
+            pltpu.SemaphoreType.DMA((3, N)),
+        ],
+        compiler_params=pltpu.CompilerParams(
+            collective_id=0, has_side_effects=True, vmem_limit_bytes=40 * 1024 * 1024
+        ),
+    )(embeddings, labels.reshape(1, IMGS), weights, strength.reshape(1, 1))
+    return new_weights, losses.reshape(IMGS)
+
+
+def general(embeddings, labels, weights, strength):
     lam = 16.0 * 0.01 * jnp.exp2(strength[0].astype(jnp.float32))
     full_x = lax.all_gather(embeddings, "cls", axis=1, tiled=True)
     cls_width = weights.shape[1]
@@ -26,7 +331,7 @@
     operand = master.astype(jnp.bfloat16)
     losses = jnp.zeros((labels.shape[0],), jnp.float32)
     for step in range(ITERS):
-        logits = jnp.dot(full_x, operand, preferred_element_type=jnp.float32) * scale
+        logits = jnp.dot(full_x, operand, preferred_element_type=jnp.float32) * SCALE
         local_top = jnp.max(logits, axis=1)
         label_term = jnp.sum(logits * onehot, axis=1)
         top = lax.pmax(local_top, "cls")
@@ -40,7 +345,7 @@
             lax.dot_general(
                 full_x, resid, (((0,), (0,)), ((), ())), preferred_element_type=jnp.float32
             )
-            * scale
+            * SCALE
         )
         grad = lax.psum(grad_local, "img")
         master = shrink(master, grad, lam)
@@ -53,7 +358,7 @@
 def solution(mesh):
     placed = (P(("grp", "img"), "cls"), P(("grp", "img")), P(("grp", "img"), "cls"), P("grp"))
     return jax.shard_map(
-        shards,
+        fused if mesh.shape["cls"] == N else general,
         mesh=mesh,
         in_specs=placed,
         out_specs=(P(("grp", "img"), "cls"), P(("grp", "img"))),

time: 211 us -> 61.2 us (0.29)
  waiting for transfers between devices: 111 us -> 0 us
  blocking collectives: 64.2 us -> 0 us
  Pallas kernels: 0 us -> 57.1 us
  between operations: 14.5 us -> 1.32 us
  matrix products: 11.3 us -> 0 us
  other arithmetic: 5.92 us -> 0 us
    all_gather x1 -> x0, waiting for transfers between devices: 60.3 us -> none  [shards(): full_x = lax.all_gather(embeddings, 'cls', axis=1, tiled=True)]
    pallas_call x0 -> x1, Pallas kernels: none -> 57.1 us  [fused(): pl.pallas_call(kernel, out_shape=(jax.ShapeDtypeStruct((768, CLS), f32),...]
    psum x2 -> x0, waiting for transfers between devices: 50.1 us -> none  [shards(): grad = lax.psum(grad_local, 'img')]
    pmax x2 -> x0, blocking collectives: 34.1 us -> none  [shards(): top = lax.pmax(local_top, 'cls')]
    psum x2 -> x0, blocking collectives: 27.6 us -> none  [shards(): lax.psum((jnp.sum(jnp.exp(logits - top[:, None]), axis=1), label_term), '...]
    dot_general x4 -> x0, matrix products: 11.3 us -> none  [the longest x2 6.26 us: shards(): lax.dot_general(full_x, resid, (((0,), (0,)), ((), ())), preferred_elemen...]
    mul x2 -> x0, other arithmetic: 2.99 us -> none  [shrink(): return jnp.sign(moved) * jnp.maximum(jnp.abs(moved) - lam, 0.0)]
    all_gather x1 -> x0, blocking collectives: 2.5 us -> none  [shards(): master = lax.all_gather(weights, 'img', axis=0, tiled=True)]
  transfers between devices with their start and end apart: 3 -> 0, of which waited for: 3 -> 0; matrix products, arithmetic and copies ran while one was open for 1% -> 0% of each run, Pallas kernels for 0% -> 0%
where the time goes in v1:
time: 61.2 us; the launch traced here: 61 us
  Pallas kernels  57.1 us (93%)
  local copies, waits for them, and re-layouts  2.6 us (4%)
  between operations  1.32 us (2%)
    pallas_call x1, Pallas kernels, fused(): pl.pallas_call(kernel, out_shape=(jax.ShapeDtypeStruct((768, CLS), f32),...  57.1 us
    unnamed x7, local copies, waits for them, and re-layouts  2.6 us

profile of v1, /device:TPU:1, one launch (start us, length us, event | category | flops | bytes accessed | tf_op | source)
XLA Modules:
  0.0 61.0 jit_solution(751334069451044261)
XLA Ops:
  1.3 0.0 copy-start
  1.3 0.0 copy-start.1
  1.3 1.2 %copy.6.x_ref = bf16[1024,192]{1,0:T(8,128)(2,1)S(1)} copy(bf16[1024,192]{0,1:T(8,128)(2,1)} %param.4) | data formatting | bytes 786432 | tf_op args[0]
  2.5 0.0 copy-done
  2.6 0.0 copy-done.1
  2.6 57.1 %shard_map.59 = (f32[768,128]{1,0:T(8,128)S(1)}, f32[1,1024]{1,0:T(1,128)S(1)}) custom-call(bf16[1024,192]{1,0:T(8,128)(2,1)S(1)} %copy.6.x_ref, s32[1,1024]{1,0:T(1,128)S(1)} %bitcast.4, f32[768,128]{1,0:T(8,128)S(1)} %copy-done, s32[1,1]{1,0:T(1,128)} %bitcast.3.s_ref), custom_call_target="tpu_custom_call" | custom-call | tf_op jit(solution)/shard_map/pallas_call | solution.py:286
  59.7 0.7 %copy.10 = f32[768,128]{1,0:T(8,128)} copy(f32[768,128]{1,0:T(8,128)S(1)} %get-tuple-element.8) | data formatting | bytes 786432
  60.4 0.6 copy.11
Async XLA Ops:
  1.3 1.3 %copy-start = (f32[768,128]{1,0:T(8,128)S(1)}, f32[768,128]{1,0:T(8,128)}, u32[]{:S(2)}) copy-start(f32[768,128]{1,0:T(8,128)} %w_ref.1) | copy-start | bytes 1179652
  1.3 1.3 %copy-start.1 = (s32[1024]{0:T(1024)S(1)}, s32[1024]{0:T(1024)}, u32[]{:S(2)}) copy-start(s32[1024]{0:T(1024)} %param.5) | copy-start | bytes 12292

commit v2 on v1

v2 whole, which is shorter than its diff:
```python
import functools
import math

import jax
import jax.numpy as jnp
from jax import lax
from jax.experimental import pallas as pl
from jax.experimental.pallas import tpu as pltpu
from jax.sharding import PartitionSpec as P

D = 1536
ITERS = 2
MESH = pl.DeviceIdType.MESH
SCALE = 1.0 / math.sqrt(D)

NX, NZ = 2, 4
N = NX * NZ
IMGS, WIDTH, CLS = 1024, 192, 128
UP, DOWN, ACROSS = 0, 1, 2
PARTS = ((0, 96), (96, 64), (160, 32))
LAST = len(PARTS) - 1
CHUNK = 256


def shrink(master, grad, lam):
    moved = master - 16.0 * grad
    return jnp.sign(moved) * jnp.maximum(jnp.abs(moved) - lam, 0.0)


def kernel(x_hbm, lab_ref, w_hbm, s_ref, out_ref, loss_ref,
           w_ref, load, xd, wb, wb2, acc, ex, resid, gsend, grecv, lses, picks,
           send_sem, recv_sem, w_send, w_recv, g_send, g_recv, l_send, l_recv):
    me = lax.axis_index("cls")
    img = lax.axis_index("img")
    grp = lax.axis_index("grp")
    z, x = me // NX, me % NX
    mate = (grp, me, 1 - img)
    has_up, has_down = z < NZ - 1, z > 0
    yes = z >= 0

    def rows(at, n):
        return pl.ds(pl.multiple_of(at, 16), n)

    loads = [
        pltpu.make_async_copy(x_hbm, xd.at[rows(me * WIDTH, WIDTH)], load.at[0]),
        pltpu.make_async_copy(w_hbm, w_ref, load.at[1]),
    ]
    for c in loads:
        c.start()
    barrier = pltpu.get_barrier_semaphore()
    pl.semaphore_signal(barrier, inc=1, device_id=mate, device_id_type=MESH)
    pl.semaphore_signal(
        barrier, inc=1, device_id=(grp, z * NX + 1 - x, img), device_id_type=MESH)

    @pl.when(has_up)
    def _():
        pl.semaphore_signal(barrier, inc=1, device_id=(grp, me + NX, img), device_id_type=MESH)

    @pl.when(has_down)
    def _():
        pl.semaphore_signal(barrier, inc=1, device_id=(grp, me - NX, img), device_id_type=MESH)

    def place(sz, sx, q):
        at, n = PARTS[q]
        return xd.at[rows((sz * NX + sx) * WIDTH + at, n)]

    def copy(sz, sx, q, way):
        to = {UP: me + NX, DOWN: me - NX, ACROSS: z * NX + 1 - x}[way]
        ref = place(sz, sx, q)
        return pltpu.make_async_remote_copy(
            src_ref=ref,
            dst_ref=ref,
            send_sem=send_sem.at[way, sz * NX + sx, q],
            recv_sem=recv_sem.at[sz * NX + sx, q],
            device_id=(grp, to, img),
            device_id_type=MESH,
        )

    started = []

    def send(cond, *args):
        @pl.when(cond)
        def _():
            copy(*args).start()
        started.append((cond, args))

    def arrived(sz, sx, q):
        copy(sz, sx, q, ACROSS).wait_recv()

    def put_weights(buf, values):
        for j in range(2):
            buf[img * 2 + j] = values[384 * j:384 * j + 384].T.astype(jnp.bfloat16)

    loads[1].wait()
    put_weights(wb, w_ref[...])
    acc[...] = jnp.zeros_like(acc)
    loads[0].wait()
    pl.semaphore_wait(barrier, 2 + has_up.astype(jnp.int32) + has_down.astype(jnp.int32))
    send(yes, z, x, LAST, ACROSS)
    for q in range(LAST):
        send(has_up, z, x, q, UP)
        send(has_down, z, x, q, DOWN)
        send(yes, z, x, q, ACROSS)

    def weights_copy(buf, step):
        half = buf.at[pl.ds(img * 2, 2)]
        return pltpu.make_async_remote_copy(
            src_ref=half, dst_ref=half, send_sem=w_send.at[step], recv_sem=w_recv.at[step],
            device_id=mate, device_id_type=MESH)

    def weights_arrived(buf, step):
        half = buf.at[pl.ds((1 - img) * 2, 2)]
        pltpu.make_async_remote_copy(
            src_ref=half, dst_ref=half, send_sem=w_send.at[step], recv_sem=w_recv.at[step],
            device_id=mate, device_id_type=MESH).wait_recv()

    weights_copy(wb, 0).start()

    def add_group(sz):
        for n in range(0, IMGS, CHUNK):
            r = slice(n, n + CHUNK)
            acc[:, r] += jnp.dot(
                wb[sz], xd[rows(sz * 384, 384), r], preferred_element_type=jnp.float32)

    def half_logits(h, r):
        w = jnp.concatenate([wb2[2 * h], wb2[2 * h + 1]], axis=1)
        return jnp.dot(w, xd[rows(h * 768, 768), r], preferred_element_type=jnp.float32)

    def finish(sz):
        for q in range(LAST):
            arrived(sz, 1 - x, q)
        add_group(sz)

    def sides(d):
        return (
            (z - d, z >= d, UP, has_up),
            (z + d, z + d < NZ, DOWN, has_down),
        )

    for d in range(NZ):
        if d > 0:
            for q in range(LAST):
                for sz, here, way, onward in sides(d):
                    @pl.when(here)
                    def _(sz=sz, q=q):
                        arrived(sz, x, q)
                    send(jnp.logical_and(here, onward), sz, x, q, way)
                    send(here, sz, x, q, ACROSS)
        else:
            arrived(z, 1 - x, LAST)
        for sx in (x, 1 - x):
            send(jnp.logical_and(z == d, has_up), z, sx, LAST, UP)
            send(jnp.logical_and(NZ - 1 - z == d, has_down), z, sx, LAST, DOWN)
        if d == 1:
            weights_arrived(wb, 0)
            finish(z)
    for d in range(1, NZ):
        for sz, here, way, onward in sides(d):
            for sx in (x, 1 - x):
                @pl.when(here)
                def _(sz=sz, sx=sx):
                    arrived(sz, sx, LAST)
                send(jnp.logical_and(here, onward), sz, sx, LAST, way)
        for sz, here, _, _ in sides(d - 1) if d > 1 else ():
            @pl.when(here)
            def _(sz=sz):
                finish(sz)

    for sz, here, _, _ in sides(NZ - 1):
        @pl.when(here)
        def _(sz=sz):
            finish(sz)

    lam = 0.16 * jnp.exp2(s_ref[...].astype(jnp.float32))
    first = me * CLS

    def stat_copy(buf, sems, k):
        return pltpu.make_async_remote_copy(
            src_ref=buf.at[me], dst_ref=buf.at[me],
            send_sem=l_send.at[sems, k], recv_sem=l_recv.at[sems, me],
            device_id=(grp, (me + k) % N, img), device_id_type=MESH)

    def stat_arrived(buf, sems, k):
        frm = (me + k) % N
        pltpu.make_async_remote_copy(
            src_ref=buf.at[frm], dst_ref=buf.at[frm],
            send_sem=l_send.at[sems, k], recv_sem=l_recv.at[sems, frm],
            device_id=(grp, frm, img), device_id_type=MESH).wait_recv()

    def grad_copy(step, j):
        return pltpu.make_async_remote_copy(
            src_ref=gsend.at[step, j], dst_ref=grecv.at[step, j],
            send_sem=g_send.at[step, j], recv_sem=g_recv.at[step, j],
            device_id=mate, device_id_type=MESH)

    def grad_part(h, j):
        return lax.dot_general(
            xd[rows(h * 768 + j * 256, 256), :], resid[...], (((1,), (1,)), ((), ())),
            preferred_element_type=jnp.float32)

    for step in range(ITERS):
        last = step == ITERS - 1
        tops = []
        lse_buf = lses.at[step]
        if step > 0:
            weights_arrived(wb2, 1)
        for n in range(0, IMGS, CHUNK):
            r = slice(n, n + CHUNK)
            logits = acc[:, r] * SCALE
            if step > 0:
                logits = (acc[:, r] + half_logits(1 - img, r)) * SCALE
            top = jnp.max(logits, axis=0, keepdims=True)
            e = jnp.exp(logits - top)
            ex[:, r] = e
            lse_buf[me, :, r] = top + jnp.log(jnp.sum(e, axis=0, keepdims=True))
            tops.append(top)
            if last:
                hot = lab_ref[:, r] == first + lax.broadcasted_iota(jnp.int32, (CLS, CHUNK), 0)
                picks[me, :, r] = jnp.sum(jnp.where(hot, logits, 0.0), axis=0, keepdims=True)
        for k in range(1, N):
            stat_copy(lse_buf, step, k).start()
        if last:
            for k in range(1, N):
                stat_copy(picks, 2, k).start()
        for k in range(1, N):
            stat_arrived(lse_buf, step, k)
        for n in range(0, IMGS, CHUNK):
            r = slice(n, n + CHUNK)
            parts = [lse_buf[k, :, r] for k in range(N)]
            top = functools.reduce(jnp.maximum, parts)
            lse = top + jnp.log(sum(jnp.exp(p - top) for p in parts))
            if last:
                loss_ref[:, r] = lse
            hot = lab_ref[:, r] == first + lax.broadcasted_iota(jnp.int32, (CLS, CHUNK), 0)
            prob = ex[:, r] * jnp.exp(tops[n // CHUNK] - lse)
            resid[:, r] = (prob - jnp.where(hot, 1.0, 0.0)).astype(jnp.bfloat16)
        for j in range(3):
            gsend[step, j] = grad_part(1 - img, j)
            grad_copy(step, j).start()
        for j in range(3):
            r = slice(256 * j, 256 * j + 256)
            grad = grad_part(img, j)
            grad_copy(step, j).wait_recv()
            moved = w_ref[r] - 16.0 * ((grad + grecv[step, j]) * SCALE)
            new = moved - jnp.clip(moved, -lam, lam)
            if last:
                out_ref[r] = new
            else:
                w_ref[r] = new
        if not last:
            put_weights(wb2, w_ref[...])
            weights_copy(wb2, 1).start()
            for n in range(0, IMGS, CHUNK):
                acc[:, n:n + CHUNK] = half_logits(img, slice(n, n + CHUNK))

    for k in range(1, N):
        stat_arrived(picks, 2, k)
    loss_ref[...] = loss_ref[...] - sum(picks[k] for k in range(N))

    for cond, args in started:
        @pl.when(cond)
        def _(args=args):
            copy(*args).wait_send()
    weights_copy(wb, 0).wait_send()
    weights_copy(wb2, 1).wait_send()
    for step in range(ITERS):
        for j in range(3):
            grad_copy(step, j).wait_send()
        for k in range(1, N):
            stat_copy(lses.at[step], step, k).wait_send()
    for k in range(1, N):
        stat_copy(picks, 2, k).wait_send()


def fused(embeddings, labels, weights, strength):
    vmem = pl.BlockSpec(memory_space=pltpu.VMEM)
    hbm = pl.BlockSpec(memory_space=pl.ANY)
    f32, bf16 = jnp.float32, jnp.bfloat16
    new_weights, losses = pl.pallas_call(
        kernel,
        out_shape=(
            jax.ShapeDtypeStruct((768, CLS), f32),
            jax.ShapeDtypeStruct((1, IMGS), f32),
        ),
        in_specs=[hbm, vmem, hbm, vmem],
        out_specs=(vmem, vmem),
        scratch_shapes=[
            pltpu.VMEM((768, CLS), f32),
            pltpu.SemaphoreType.DMA((2,)),
            pltpu.VMEM((D, IMGS), bf16),
            pltpu.VMEM((4, CLS, 384), bf16),
            pltpu.VMEM((4, CLS, 384), bf16),
            pltpu.VMEM((CLS, IMGS), f32),
            pltpu.VMEM((CLS, IMGS), f32),
            pltpu.VMEM((CLS, IMGS), bf16),
            pltpu.VMEM((ITERS, 3, 256, CLS), f32),
            pltpu.VMEM((ITERS, 3, 256, CLS), f32),
            pltpu.VMEM((ITERS, N, 1, IMGS), f32),
            pltpu.VMEM((N, 1, IMGS), f32),
            pltpu.SemaphoreType.DMA((3, N, len(PARTS))),
            pltpu.SemaphoreType.DMA((N, len(PARTS))),
            pltpu.SemaphoreType.DMA((2,)),
            pltpu.SemaphoreType.DMA((2,)),
            pltpu.SemaphoreType.DMA((2, 3)),
            pltpu.SemaphoreType.DMA((2, 3)),
            pltpu.SemaphoreType.DMA((3, N)),
            pltpu.SemaphoreType.DMA((3, N)),
        ],
        compiler_params=pltpu.CompilerParams(
            collective_id=0, has_side_effects=True, vmem_limit_bytes=60 * 1024 * 1024
        ),
    )(embeddings.T, labels.reshape(1, IMGS), weights, strength.reshape(1, 1))
    return new_weights, losses.reshape(IMGS)


def general(embeddings, labels, weights, strength):
    lam = 16.0 * 0.01 * jnp.exp2(strength[0].astype(jnp.float32))
    full_x = lax.all_gather(embeddings, "cls", axis=1, tiled=True)
    cls_width = weights.shape[1]
    first_class = lax.axis_index("cls") * cls_width
    classes = first_class + lax.iota(jnp.int32, cls_width)
    onehot = (labels[:, None] == classes[None, :]).astype(jnp.float32)
    master = lax.all_gather(weights, "img", axis=0, tiled=True)
    operand = master.astype(jnp.bfloat16)
    losses = jnp.zeros((labels.shape[0],), jnp.float32)
    for step in range(ITERS):
        logits = jnp.dot(full_x, operand, preferred_element_type=jnp.float32) * SCALE
        local_top = jnp.max(logits, axis=1)
        label_term = jnp.sum(logits * onehot, axis=1)
        top = lax.pmax(local_top, "cls")
        total, picked = lax.psum(
            (jnp.sum(jnp.exp(logits - top[:, None]), axis=1), label_term), "cls"
        )
        lse = top + jnp.log(total)
        losses = lse - picked
        resid = (jnp.exp(logits - lse[:, None]) - onehot).astype(jnp.bfloat16)
        grad_local = (
            lax.dot_general(
                full_x, resid, (((0,), (0,)), ((), ())), preferred_element_type=jnp.float32
            )
            * SCALE
        )
        grad = lax.psum(grad_local, "img")
        master = shrink(master, grad, lam)
        operand = master.astype(jnp.bfloat16)
    rows = weights.shape[0]
    new_weights = lax.dynamic_slice_in_dim(master, lax.axis_index("img") * rows, rows, 0)
    return (new_weights, losses)


def solution(mesh):
    placed = (P(("grp", "img"), "cls"), P(("grp", "img")), P(("grp", "img"), "cls"), P("grp"))
    return jax.shard_map(
        fused if mesh.shape["cls"] == N else general,
        mesh=mesh,
        in_specs=placed,
        out_specs=(P(("grp", "img"), "cls"), P(("grp", "img"))),
        check_vma=False,
    )
```

time: 61.2 us -> 57.5 us (0.940)
  Pallas kernels: 57.1 us -> 53.7 us
    pallas_call x1, Pallas kernels: 57.1 us -> 53.7 us  [fused(): pl.pallas_call(kernel, out_shape=(jax.ShapeDtypeStruct((768, CLS), f32),...]
    unnamed x7 -> x4, local copies, waits for them, and re-layouts: 2.6 us -> 2.37 us
where the time goes in v2:
time: 57.5 us; the launch traced here: 57.3 us
  Pallas kernels  53.7 us (93%)
  local copies, waits for them, and re-layouts  2.37 us (4%)
  between operations  1.29 us (2%)
    pallas_call x1, Pallas kernels, fused(): pl.pallas_call(kernel, out_shape=(jax.ShapeDtypeStruct((768, CLS), f32),...  53.7 us
    unnamed x4, local copies, waits for them, and re-layouts  2.37 us

profile of v2, /device:TPU:1, one launch (start us, length us, event | category | flops | bytes accessed | tf_op | source)
XLA Modules:
  0.0 57.3 jit_solution(11369995979874026227)
XLA Ops:
  1.3 53.7 %shard_map.59 = (f32[768,128]{1,0:T(8,128)}, f32[1,1024]{1,0:T(1,128)}) custom-call(bf16[192,1024]{1,0:T(8,128)(2,1)} %bitcast.5, s32[1,1024]{1,0:T(1,128)} %bitcast.6, f32[768,128]{1,0:T(8,128)} %w_hbm.1, s32[1,1]{1,0:T(1,128)} %bitcast.4.s_ref), custom_call_target="tpu_custom_call" | custom-call | tf_op jit(solution)/shard_map/pallas_call | solution.py:279
  55.0 0.0 copy-start
  55.0 1.8 %copy.9 = f32[768,128]{1,0:T(8,128)} copy(f32[768,128]{1,0:T(8,128)} %get-tuple-element.8) | data formatting | bytes 786432
  56.7 0.0 copy-done
  56.7 0.6 %copy.10 = f32[1024]{0:T(1024)} copy(f32[1024]{0:T(1024)S(1)} %bitcast.7) | data formatting | bytes 8192
Async XLA Ops:
  55.0 1.8 %copy-start = (f32[1,1024]{1,0:T(1,128)S(1)}, f32[1,1024]{1,0:T(1,128)}, u32[]{:S(2)}) copy-start(f32[1,1024]{1,0:T(1,128)} %get-tuple-element.5) | copy-start | bytes 12292

commit v3 on v2

--- a/solution.py
+++ b/solution.py
@@ -201,7 +201,7 @@
     for step in range(ITERS):
         last = step == ITERS - 1
         tops = []
-        lse_buf = lses.at[step]
+        lse_buf = (lses, picks)[step]
         if step > 0:
             weights_arrived(wb2, 1)
         for n in range(0, IMGS, CHUNK):
@@ -212,25 +212,22 @@
             top = jnp.max(logits, axis=0, keepdims=True)
             e = jnp.exp(logits - top)
             ex[:, r] = e
-            lse_buf[me, :, r] = top + jnp.log(jnp.sum(e, axis=0, keepdims=True))
+            lse_buf[me, 0:1, r] = top + jnp.log(jnp.sum(e, axis=0, keepdims=True))
             tops.append(top)
             if last:
                 hot = lab_ref[:, r] == first + lax.broadcasted_iota(jnp.int32, (CLS, CHUNK), 0)
-                picks[me, :, r] = jnp.sum(jnp.where(hot, logits, 0.0), axis=0, keepdims=True)
+                picks[me, 1:2, r] = jnp.sum(jnp.where(hot, logits, 0.0), axis=0, keepdims=True)
         for k in range(1, N):
             stat_copy(lse_buf, step, k).start()
-        if last:
-            for k in range(1, N):
-                stat_copy(picks, 2, k).start()
         for k in range(1, N):
             stat_arrived(lse_buf, step, k)
         for n in range(0, IMGS, CHUNK):
             r = slice(n, n + CHUNK)
-            parts = [lse_buf[k, :, r] for k in range(N)]
+            parts = [lse_buf[k, 0:1, r] for k in range(N)]
             top = functools.reduce(jnp.maximum, parts)
             lse = top + jnp.log(sum(jnp.exp(p - top) for p in parts))
             if last:
-                loss_ref[:, r] = lse
+                loss_ref[:, r] = lse - sum(picks[k, 1:2, r] for k in range(N))
             hot = lab_ref[:, r] == first + lax.broadcasted_iota(jnp.int32, (CLS, CHUNK), 0)
             prob = ex[:, r] * jnp.exp(tops[n // CHUNK] - lse)
             resid[:, r] = (prob - jnp.where(hot, 1.0, 0.0)).astype(jnp.bfloat16)
@@ -253,10 +250,6 @@
             for n in range(0, IMGS, CHUNK):
                 acc[:, n:n + CHUNK] = half_logits(img, slice(n, n + CHUNK))
 
-    for k in range(1, N):
-        stat_arrived(picks, 2, k)
-    loss_ref[...] = loss_ref[...] - sum(picks[k] for k in range(N))
-
     for cond, args in started:
         @pl.when(cond)
         def _(args=args):
@@ -267,9 +260,7 @@
         for j in range(3):
             grad_copy(step, j).wait_send()
         for k in range(1, N):
-            stat_copy(lses.at[step], step, k).wait_send()
-    for k in range(1, N):
-        stat_copy(picks, 2, k).wait_send()
+            stat_copy((lses, picks)[step], step, k).wait_send()
 
 
 def fused(embeddings, labels, weights, strength):
@@ -295,16 +286,16 @@
             pltpu.VMEM((CLS, IMGS), bf16),
             pltpu.VMEM((ITERS, 3, 256, CLS), f32),
             pltpu.VMEM((ITERS, 3, 256, CLS), f32),
-            pltpu.VMEM((ITERS, N, 1, IMGS), f32),
             pltpu.VMEM((N, 1, IMGS), f32),
+            pltpu.VMEM((N, 2, IMGS), f32),
             pltpu.SemaphoreType.DMA((3, N, len(PARTS))),
             pltpu.SemaphoreType.DMA((N, len(PARTS))),
             pltpu.SemaphoreType.DMA((2,)),
             pltpu.SemaphoreType.DMA((2,)),
             pltpu.SemaphoreType.DMA((2, 3)),
             pltpu.SemaphoreType.DMA((2, 3)),
-            pltpu.SemaphoreType.DMA((3, N)),
-            pltpu.SemaphoreType.DMA((3, N)),
+            pltpu.SemaphoreType.DMA((ITERS, N)),
+            pltpu.SemaphoreType.DMA((ITERS, N)),
         ],
         compiler_params=pltpu.CompilerParams(
             collective_id=0, has_side_effects=True, vmem_limit_bytes=60 * 1024 * 1024

time: 57.5 us -> 57.5 us (level)
  no operation moved by 1% of the time
where the time goes in v3:
time: 57.5 us; the launch traced here: 57.3 us
  Pallas kernels  53.7 us (93%)
  local copies, waits for them, and re-layouts  2.37 us (4%)
  between operations  1.29 us (2%)
    pallas_call x1, Pallas kernels, fused(): pl.pallas_call(kernel, out_shape=(jax.ShapeDtypeStruct((768, CLS), f32),...  53.7 us
    unnamed x4, local copies, waits for them, and re-layouts  2.37 us

profile of v3, /device:TPU:1, one launch (start us, length us, event | category | flops | bytes accessed | tf_op | source)
XLA Modules:
  0.0 57.3 jit_solution(130967370220632468)
XLA Ops:
  1.3 53.7 %shard_map.59 = (f32[768,128]{1,0:T(8,128)}, f32[1,1024]{1,0:T(1,128)}) custom-call(bf16[192,1024]{1,0:T(8,128)(2,1)} %bitcast.5, s32[1,1024]{1,0:T(1,128)} %bitcast.6, f32[768,128]{1,0:T(8,128)} %w_hbm.1, s32[1,1]{1,0:T(1,128)} %bitcast.4.s_ref), custom_call_target="tpu_custom_call" | custom-call | tf_op jit(solution)/shard_map/pallas_call | solution.py:270
  54.9 0.0 copy-start
  54.9 1.8 %copy.9 = f32[768,128]{1,0:T(8,128)} copy(f32[768,128]{1,0:T(8,128)} %get-tuple-element.8) | data formatting | bytes 786432
  56.7 0.0 copy-done
  56.7 0.6 %copy.10 = f32[1024]{0:T(1024)} copy(f32[1024]{0:T(1024)S(1)} %bitcast.7) | data formatting | bytes 8192
Async XLA Ops:
  54.9 1.8 %copy-start = (f32[1,1024]{1,0:T(1,128)S(1)}, f32[1,1024]{1,0:T(1,128)}, u32[]{:S(2)}) copy-start(f32[1,1024]{1,0:T(1,128)} %get-tuple-element.5) | copy-start | bytes 12292

commit v4 on v3

--- a/solution.py
+++ b/solution.py
@@ -227,7 +227,10 @@
             top = functools.reduce(jnp.maximum, parts)
             lse = top + jnp.log(sum(jnp.exp(p - top) for p in parts))
             if last:
-                loss_ref[:, r] = lse - sum(picks[k, 1:2, r] for k in range(N))
+                loss = lse - sum(picks[k, 1:2, r] for k in range(N))
+                for i in range(0, CHUNK, 128):
+                    row = (n + i) // 128
+                    loss_ref[row:row + 1, :] = loss[:, i:i + 128]
             hot = lab_ref[:, r] == first + lax.broadcasted_iota(jnp.int32, (CLS, CHUNK), 0)
             prob = ex[:, r] * jnp.exp(tops[n // CHUNK] - lse)
             resid[:, r] = (prob - jnp.where(hot, 1.0, 0.0)).astype(jnp.bfloat16)
@@ -271,7 +274,7 @@
         kernel,
         out_shape=(
             jax.ShapeDtypeStruct((768, CLS), f32),
-            jax.ShapeDtypeStruct((1, IMGS), f32),
+            jax.ShapeDtypeStruct((IMGS // 128, 128), f32),
         ),
         in_specs=[hbm, vmem, hbm, vmem],
         out_specs=(vmem, vmem),

time: 57.5 us -> 57.5 us (level)
  no operation moved by 1% of the time
where the time goes in v4:
time: 57.5 us; the launch traced here: 57.3 us
  Pallas kernels  53.7 us (93%)
  local copies, waits for them, and re-layouts  2.37 us (4%)
  between operations  1.29 us (2%)
    pallas_call x1, Pallas kernels, fused(): pl.pallas_call(kernel, out_shape=(jax.ShapeDtypeStruct((768, CLS), f32),...  53.7 us
    unnamed x4, local copies, waits for them, and re-layouts  2.37 us

profile of v4, /device:TPU:1, one launch (start us, length us, event | category | flops | bytes accessed | tf_op | source)
XLA Modules:
  0.0 57.3 jit_solution(405446131818300417)
XLA Ops:
  1.3 53.7 %shard_map.59 = (f32[768,128]{1,0:T(8,128)}, f32[8,128]{1,0:T(8,128)}) custom-call(bf16[192,1024]{1,0:T(8,128)(2,1)} %bitcast.5, s32[1,1024]{1,0:T(1,128)} %bitcast.6, f32[768,128]{1,0:T(8,128)} %w_hbm.1, s32[1,1]{1,0:T(1,128)} %bitcast.4.s_ref), custom_call_target="tpu_custom_call" | custom-call | tf_op jit(solution)/shard_map/pallas_call | solution.py:273
  54.9 0.0 copy-start
  54.9 1.8 %copy.9 = f32[768,128]{1,0:T(8,128)} copy(f32[768,128]{1,0:T(8,128)} %get-tuple-element.8) | data formatting | bytes 786432
  56.7 0.0 copy-done
  56.7 0.6 %copy.10 = f32[1024]{0:T(1024)} copy(f32[1024]{0:T(1024)S(1)} %bitcast.7) | data formatting | bytes 8192
Async XLA Ops:
  54.9 1.8 %copy-start = (f32[8,128]{1,0:T(8,128)S(1)}, f32[8,128]{1,0:T(8,128)}, u32[]{:S(2)}) copy-start(f32[8,128]{1,0:T(8,128)} %get-tuple-element.5) | copy-start | bytes 12292
